TPU v7x, 32 devices: a whole 2x2x4 slice. The times are simulated.
32 devices in a mesh: scen: 4 (over x, core), wide: 8 (over z, y).
Axes of the slice: x: 2, y: 2, z: 4, core: 2. Of those that a mesh axis runs over, the one named last changes fastest.
Arguments:
- hess_scen: float32 [32, 512, 512], P(('scen', 'wide')), may hold values from -1.5 to 5.5, as said below
- upper_flags: int32 [32, 512], P(('scen', 'wide')), may hold values 0 or 1
- lower_dual: float32 [32, 512], P(('scen', 'wide')), may hold values from 0.1 to 10
- lower_slack: float32 [32, 512], P(('scen', 'wide')), may hold values from 0.1 to 10
- upper_dual: float32 [32, 512], P(('scen', 'wide')), may hold values from 0.1 to 10
- upper_slack: float32 [32, 512], P(('scen', 'wide')), may hold values from 0.1 to 10
- coupling: float32 [32, 512, 768], P(('scen', 'wide')), may hold values from -0.25 to 0.25
- pattern: int32 [32, 32], P(('scen', 'wide')), may hold values 0 or 1
- region: int32 [32], P(('scen', 'wide')), may hold values from 0 to 31
- hess_first: float32 [768, 768], P('wide'), may hold values from -1.5 to 5.5, as said below
Outputs:
- scen_factor: float32 [32, 512, 512], P(('scen', 'wide'))
- first_factor: float32 [768, 768], P('wide')
Inputs may be any that keep to these rules, and one draw needn't show every extreme that they name: `hess_scen`: each scenario's block is symmetric positive definite. `hess_first`: symmetric positive definite.
All inputs are finite; a program needn't handle non-finite values. No bound on the sum of `upper_flags` or of `pattern` on one device may be relied on, other than what follows from the above.
Results may differ from a plain program's by a relative error of at most 0.0003.
Values sent between devices are 32-bit elements; how exact they have to be, the bound alone decides.
No kernel may reach another device: no remote copies, remote signals or barrier semaphores. Data moves between devices by JAX's collectives and lax.ppermute only.
A program may use at most 64 MiB of HBM per device.

v0:
```python
import jax
import jax.numpy as jnp
from jax import lax
from jax.sharding import PartitionSpec as P

N0 = 768
PW = 256


def gather_panel(columns):
    return lax.all_gather(columns, "wide", axis=0, tiled=True)


def lower_solve(factor, rows):
    return jax.scipy.linalg.solve_triangular(factor, rows.T, lower=True).T


def per_device(
    hess_scen,
    upper_flags,
    lower_dual,
    lower_slack,
    upper_dual,
    upper_slack,
    coupling,
    pattern,
    region,
    hess_first,
):
    order = hess_scen.shape[1]
    barrier = lower_dual / lower_slack + upper_flags.astype(jnp.float32) * upper_dual / upper_slack
    block = hess_scen + barrier[:, :, None] * jnp.eye(order, dtype=jnp.float32)[None, :, :]
    factor = jnp.linalg.cholesky(block)
    blocks = pattern.shape[1]
    width = N0 // blocks
    home = (region[:, None] == jnp.arange(blocks, dtype=jnp.int32)[None, :]).astype(jnp.int32)
    coupled = jnp.maximum(pattern, home)
    column_mask = jnp.repeat(coupled.astype(jnp.float32), width, axis=1)
    solved = jax.scipy.linalg.solve_triangular(
        factor, coupling * column_mask[:, None, :], lower=True
    )
    own_rows = hess_first.shape[0]
    whole = jnp.einsum(
        "snr,snc->rc",
        solved,
        solved,
        precision=lax.Precision.HIGHEST,
        preferred_element_type=jnp.float32,
    )
    summed = lax.psum(whole, "scen")
    local = lax.psum_scatter(summed, "wide", scatter_dimension=0, tiled=True)
    current = local + hess_first
    offset = lax.axis_index("wide") * own_rows
    row_ids = offset + jnp.arange(own_rows, dtype=jnp.int32)[:, None]
    col_ids = jnp.arange(N0, dtype=jnp.int32)[None, :]
    result = jnp.zeros((own_rows, N0), jnp.float32)
    panels = N0 // PW
    gathered = gather_panel(current[:, 0:PW])
    for step in range(panels):
        start = step * PW
        stop = start + PW
        diag_factor = jnp.linalg.cholesky(gathered[start:stop])
        own_panel = lower_solve(diag_factor, current[:, start:stop])
        result = result.at[:, start:stop].set(own_panel)
        if step + 1 < panels:
            trailing = lower_solve(diag_factor, gathered[stop:])
            update = jnp.dot(
                own_panel,
                trailing.T,
                precision=lax.Precision.HIGHEST,
                preferred_element_type=jnp.float32,
            )
            current = current.at[:, stop:].add(-update)
            gathered = gather_panel(current[:, stop : stop + PW])
    first_factor = jnp.where(row_ids >= col_ids, result, 0.0)
    return (factor, first_factor)


def solution(mesh):
    return jax.shard_map(
        per_device,
        mesh=mesh,
        in_specs=(
            P(("scen", "wide"), None, None),
            P(("scen", "wide"), None),
            P(("scen", "wide"), None),
            P(("scen", "wide"), None),
            P(("scen", "wide"), None),
            P(("scen", "wide"), None),
            P(("scen", "wide"), None, None),
            P(("scen", "wide"), None),
            P(("scen", "wide")),
            P("wide", None),
        ),
        out_specs=(P(("scen", "wide"), None, None), P("wide", None)),
        check_vma=False,
    )
```

profile of v0, /device:TPU:0, one launch (start us, length us, event | category | flops | bytes accessed | tf_op | source)
XLA Modules:
  0.0 555.2 jit_solution(12549581921355420715)
XLA Ops:
  7.3 1.6 copy.48
  9.6 11.7 %custom-call.54 = f32[1,128,128]{2,1,0:T(8,128)S(1)} custom-call(f32[1,128,128]{2,1,0:T(8,128)S(1)} %cholesky.534), custom_call_target="Cholesky" | custom-call | tf_op jit(solution)/shard_map/jit(cholesky)/cholesky | solution.py:33
  21.5 9.8 %custom-call.55 = f32[1,1,128,128]{2,3,1,0:T(8,128)S(1)} custom-call(f32[1,1,128,128]{3,2,1,0:T(8,128)S(1)} %get-tuple-element.194), custom_call_target="InvertDiagBlocksLowerTriangular" | custom-call | tf_op jit(solution)/shard_map/jit(cholesky)/cholesky | solution.py:33
  32.1 11.7 %custom-call.56 = f32[1,128,128]{2,1,0:T(8,128)S(1)} custom-call(f32[1,128,128]{2,1,0:T(8,128)S(1)} %cholesky.538), custom_call_target="Cholesky" | custom-call | tf_op jit(solution)/shard_map/jit(cholesky)/cholesky | solution.py:33
  44.1 10.0 %custom-call.57 = f32[1,1,128,128]{2,3,1,0:T(8,128)S(1)} custom-call(f32[1,1,128,128]{3,2,1,0:T(8,128)S(1)} %get-tuple-element.192), custom_call_target="InvertDiagBlocksLowerTriangular" | custom-call | tf_op jit(solution)/shard_map/jit(cholesky)/cholesky | solution.py:33
  55.0 11.7 %custom-call.58 = f32[1,128,128]{2,1,0:T(8,128)S(1)} custom-call(f32[1,128,128]{2,1,0:T(8,128)S(1)} %cholesky.543), custom_call_target="Cholesky" | custom-call | tf_op jit(solution)/shard_map/jit(cholesky)/cholesky | solution.py:33
  66.8 9.8 %custom-call.59 = f32[1,1,128,128]{2,3,1,0:T(8,128)S(1)} custom-call(f32[1,1,128,128]{3,2,1,0:T(8,128)S(1)} %get-tuple-element.190), custom_call_target="InvertDiagBlocksLowerTriangular" | custom-call | tf_op jit(solution)/shard_map/jit(cholesky)/cholesky | solution.py:33
  77.4 11.9 %custom-call.60 = f32[1,128,128]{2,1,0:T(8,128)S(1)} custom-call(f32[1,128,128]{2,1,0:T(8,128)S(1)} %fusion.19), custom_call_target="Cholesky" | custom-call | tf_op jit(solution)/shard_map/jit(cholesky)/cholesky | solution.py:33
  94.3 8.5 %while.14 = (s32[]{:T(128)}, f32[512,512]{0,1:T(8,128)S(1)}, s32[4,2]{0,1:T(2,128)S(1)}, f32[4,128,128]{2,1,0:T(8,128)S(1)}, s32[]{:T(128)}) while((s32[]{:T(128)}, f32[512,512]{0,1:T(8,128)S(1)}, s32[4,2]{0,1:T(2,128)S(1)}, f32[4,128,128]{2,1,0:T(8,128)S(1)}, s32[]{:T(128)}) %tuple.117), condition=%wide.while_cond.6, body=%wide.while_body.6.sunk | while | flops 2 | bytes 393321 | solution.py:39
  102.8 39.3 %custom-call.61 = f32[4,128,128]{1,2,0:T(8,128)S(1)} custom-call(f32[4,128,128]{2,1,0:T(8,128)S(1)} %get-tuple-element.79), custom_call_target="InvertDiagBlocksLowerTriangular" | custom-call | tf_op jit(solution)/shard_map/jit(_solve_triangular)/triangular_solve | solution.py:39
  143.0 1.5 broadcast_multiply_fusion
  148.6 5.8 %fusion = f32[768,768]{1,0:T(8,128)} fusion(f32[128,768]{1,0:T(8,128)S(1)} %fusion.52, f32[128,768]{1,0:T(8,128)S(1)} %fusion.53, f32[128,768]{1,0:T(8,128)S(1)} %fusion.55, f32[128,768]{1,0:T(8,128)S(1)} %fusion.27), kind=kOutput, calls=%fused_computation.8 | convolution fusion | flops 3625058304 | bytes 3932160
  154.9 72.3 %reduce-scatter.4.cloned.1.call-done = f32[96,768]{1,0:T(8,128)} async-done(((f32[768,768]{1,0:T(8,128)}), f32[96,768]{1,0:T(8,128)}) %reduce-scatter.4.cloned.1.call-update) | async-done | bytes 294928 | tf_op jit(solution)/shard_map/reduce_scatter | solution.py:51
  229.9 31.4 %all-reduce.5.cloned.1.call-done = f32[96,768]{1,0:T(8,128)} async-done(((f32[96,768]{1,0:T(8,128)}), f32[96,768]{1,0:T(8,128)}) %all-reduce.5.cloned.1.call-update) | async-done | bytes 294928 | tf_op jit(solution)/shard_map/psum | solution.py:50
  262.3 32.2 %all_gather.9 = f32[768,256]{1,0:T(8,128)S(1)} all-gather(f32[96,256]{1,0:T(8,128)S(1)} %get-tuple-element.174), channel_id=1, replica_groups=mesh['scen'=4,'wide'=8] {'wide'}, dimensions={0}, use_global_device_ids=true | all-gather | bytes 884736 | tf_op jit(solution)/shard_map/all_gather | solution.py:11
  294.8 11.7 %cholesky.436 = f32[128,128]{1,0:T(8,128)S(1)} custom-call(f32[128,128]{1,0:T(8,128)S(1)} %cholesky.547), custom_call_target="Cholesky" | custom-call | tf_op jit(solution)/shard_map/jit(cholesky)/cholesky | solution.py:62
  306.6 9.8 %custom-call.68 = f32[1,128,128]{1,2,0:T(8,128)S(1)} custom-call(f32[1,128,128]{2,1,0:T(8,128)S(1)} %get-tuple-element.188), custom_call_target="InvertDiagBlocksLowerTriangular" | custom-call | tf_op jit(solution)/shard_map/jit(cholesky)/cholesky | solution.py:62
  316.9 11.7 %cholesky.453 = f32[128,128]{1,0:T(8,128)S(1)} custom-call(f32[128,128]{1,0:T(8,128)S(1)} %convolution_subtract_fusion.7), custom_call_target="Cholesky" | custom-call | tf_op jit(solution)/shard_map/jit(cholesky)/cholesky | solution.py:62
  331.4 4.2 while.15
  335.6 19.7 %custom-call.69 = f32[2,128,128]{1,2,0:T(8,128)S(1)} custom-call(f32[2,128,128]{2,1,0:T(8,128)S(1)} %get-tuple-element.108), custom_call_target="InvertDiagBlocksLowerTriangular" | custom-call | tf_op jit(solution)/shard_map/jit(_solve_triangular)/triangular_solve | solution.py:15
  357.9 31.6 %all_gather.10 = f32[768,256]{1,0:T(8,128)S(1)} all-gather(f32[96,256]{1,0:T(8,128)S(1)} %get-tuple-element.176), channel_id=1, replica_groups=mesh['scen'=4,'wide'=8] {'wide'}, dimensions={0}, use_global_device_ids=true | all-gather | bytes 884736 | tf_op jit(solution)/shard_map/all_gather | solution.py:11
  389.7 11.7 %cholesky.470 = f32[128,128]{1,0:T(8,128)S(1)} custom-call(f32[128,128]{1,0:T(8,128)S(1)} %cholesky.550), custom_call_target="Cholesky" | custom-call | tf_op jit(solution)/shard_map/jit(cholesky)/cholesky | solution.py:62
  401.5 9.8 %custom-call.70 = f32[1,128,128]{1,2,0:T(8,128)S(1)} custom-call(f32[1,128,128]{2,1,0:T(8,128)S(1)} %get-tuple-element.184), custom_call_target="InvertDiagBlocksLowerTriangular" | custom-call | tf_op jit(solution)/shard_map/jit(cholesky)/cholesky | solution.py:62
  411.8 11.7 %cholesky.487 = f32[128,128]{1,0:T(8,128)S(1)} custom-call(f32[128,128]{1,0:T(8,128)S(1)} %convolution_subtract_fusion.6), custom_call_target="Cholesky" | custom-call | tf_op jit(solution)/shard_map/jit(cholesky)/cholesky | solution.py:62
  426.3 4.3 while.16
  430.6 19.7 %custom-call.71 = f32[2,128,128]{1,2,0:T(8,128)S(1)} custom-call(f32[2,128,128]{2,1,0:T(8,128)S(1)} %get-tuple-element.109), custom_call_target="InvertDiagBlocksLowerTriangular" | custom-call | tf_op jit(solution)/shard_map/jit(_solve_triangular)/triangular_solve | solution.py:15
  452.3 32.1 %all_gather.11 = f32[768,256]{1,0:T(8,128)S(1)} all-gather(f32[96,256]{1,0:T(8,128)S(1)} %fusion.17), channel_id=1, replica_groups=mesh['scen'=4,'wide'=8] {'wide'}, dimensions={0}, use_global_device_ids=true | all-gather | bytes 884736 | tf_op jit(solution)/shard_map/all_gather | solution.py:11
  484.6 11.7 %cholesky.504 = f32[128,128]{1,0:T(8,128)S(1)} custom-call(f32[128,128]{1,0:T(8,128)S(1)} %cholesky.553), custom_call_target="Cholesky" | custom-call | tf_op jit(solution)/shard_map/jit(cholesky)/cholesky | solution.py:62
  496.4 9.8 %custom-call.72 = f32[1,128,128]{1,2,0:T(8,128)S(1)} custom-call(f32[1,128,128]{2,1,0:T(8,128)S(1)} %get-tuple-element.180), custom_call_target="InvertDiagBlocksLowerTriangular" | custom-call | tf_op jit(solution)/shard_map/jit(cholesky)/cholesky | solution.py:62
  506.7 11.7 %cholesky.521 = f32[128,128]{1,0:T(8,128)S(1)} custom-call(f32[128,128]{1,0:T(8,128)S(1)} %convolution_subtract_fusion.5), custom_call_target="Cholesky" | custom-call | tf_op jit(solution)/shard_map/jit(cholesky)/cholesky | solution.py:62
  521.2 4.4 while.17
  525.5 19.7 %custom-call.73 = f32[2,128,128]{1,2,0:T(8,128)S(1)} custom-call(f32[2,128,128]{2,1,0:T(8,128)S(1)} %get-tuple-element.110), custom_call_target="InvertDiagBlocksLowerTriangular" | custom-call | tf_op jit(solution)/shard_map/jit(_solve_triangular)/triangular_solve | solution.py:15
  (176 shorter events, 48.6 us)
Async XLA Ops:
  7.2 1.7 copy-start.4
  7.2 1.7 copy-start.5
  7.2 1.7 copy-start.6
  7.2 1.7 copy-start.3
  7.2 1.7 copy-start.2
  7.2 220.0 %reduce-scatter.4.cloned.1.call-start = ((), (), s32[]{:S(2)}) async-start(), calls=%async_computation.2 | async-start | bytes 2654208 | tf_op jit(solution)/shard_map/reduce_scatter | solution.py:51
  94.3 48.5 %copy-start.7 = (s32[1,32]{1,0:T(1,128)S(1)}, s32[1,32]{1,0:T(1,128)}, u32[]{:S(2)}) copy-start(s32[1,32]{1,0:T(1,128)} %param.30) | copy-start | bytes 388
  154.4 106.9 %copy-start.1 = (f32[96,768]{1,0:T(8,128)S(1)}, f32[96,768]{1,0:T(8,128)}, u32[]{:S(2)}) copy-start(f32[96,768]{1,0:T(8,128)} %param.32) | copy-start | bytes 884740
  154.4 106.9 %all-reduce.5.cloned.1.call-start = ((), (), s32[]{:S(2)}) async-start(), calls=%async_computation.1 | async-start | bytes 589824 | tf_op jit(solution)/shard_map/psum | solution.py:50
  294.6 12.0 %copy-start = (f32[768,256]{1,0:T(8,128)}, f32[768,256]{1,0:T(8,128)S(1)}, u32[]{:S(2)}) copy-start(f32[768,256]{1,0:T(8,128)S(1)} %all_gather.9) | copy-start | bytes 2359300
  306.6 48.7 %slice-start = ((f32[768,256]{1,0:T(8,128)}), f32[512,256]{1,0:T(8,128)S(1)}, s32[]{:S(2)}) async-start(f32[768,256]{1,0:T(8,128)} %copy-done), calls=%async_computation.3 | async-start | bytes 1048576 | tf_op jit(solution)/shard_map/slice | solution.py:66
Sparse Core Ops, SparseCore 0:
  154.5 72.7 reduce-scatter.3
  229.6 31.6 all-reduce.4
where the time goes:
time: 564 us; the launch traced here: 555 us
  other arithmetic  288 us (51%)
  waiting for transfers between devices  104 us (18%)
  blocking collectives  96 us (17%)
  local copies, waits for them, and re-layouts  25.5 us (5%)
  between operations  22.5 us (4%)
  matrix products  18.3 us (3%)
    another operation x21, other arithmetic, per_device(): diag_factor = jnp.linalg.cholesky(gathered[start:stop])  104 us
    all_gather x3, blocking collectives, gather_panel(): return lax.all_gather(columns, 'wide', axis=0, tiled=True)  96 us
    another operation x14, other arithmetic, per_device(): factor = jnp.linalg.cholesky(block)  78.8 us
    reduce_scatter x1, waiting for transfers between devices, per_device(): local = lax.psum_scatter(summed, 'wide', scatter_dimension=0, tiled=True)  72.3 us
    another operation x7, other arithmetic, lower_solve(): return jax.scipy.linalg.solve_triangular(factor, rows.T, lower=True).T  59.1 us
    another operation x3, other arithmetic, per_device(): jax.scipy.linalg.solve_triangular(factor, coupling * column_mask[:, None,...  39.6 us
    psum x1, waiting for transfers between devices, per_device(): summed = lax.psum(whole, 'scen')  31.4 us
    another operation x22, local copies, waits for them, and re-layouts, lower_solve(): return jax.scipy.linalg.solve_triangular(factor, rows.T, lower=True).T  12.2 us
  transfers between devices with their start and end apart: 2, of which 2 were waited for; matrix products, arithmetic and copies ran while one was open for 0% of the time, Pallas kernels for 0%

commit v1 on v0

--- a/solution.py
+++ b/solution.py
@@ -47,7 +47,9 @@
         precision=lax.Precision.HIGHEST,
         preferred_element_type=jnp.float32,
     )
-    summed = lax.psum(whole, "scen")
+    summed = whole
+    for hop in (1, 2):
+        summed = summed + lax.ppermute(summed, "scen", [(dev, dev ^ hop) for dev in range(4)])
     local = lax.psum_scatter(summed, "wide", scatter_dimension=0, tiled=True)
     current = local + hess_first
     offset = lax.axis_index("wide") * own_rows

time: 564 us -> 599 us (1.062)
  waiting for transfers between devices: 104 us -> 125 us
  other arithmetic: 288 us -> 299 us
    ppermute x0 -> x2, waiting for transfers between devices: none -> 55.7 us  [per_device(): lax.ppermute(summed, 'scen', [(dev, dev ^ hop) for dev in range(4)])]
    psum x1 -> x0, waiting for transfers between devices: 31.4 us -> none  [per_device(): summed = lax.psum(whole, 'scen')]
    another operation x14, other arithmetic: 78.8 us -> 87.9 us  [per_device(): factor = jnp.linalg.cholesky(block)]
  transfers between devices with their start and end apart: 2 -> 3, of which waited for: 2 -> 3; matrix products, arithmetic and copies ran while one was open for 0% -> 0% of each run, Pallas kernels for 0% -> 0%
where the time goes in v1:
time: 599 us; the launch traced here: 590 us
  other arithmetic  299 us (50%)
  waiting for transfers between devices  125 us (21%)
  blocking collectives  97 us (16%)
  local copies, waits for them, and re-layouts  25.3 us (4%)
  between operations  22.4 us (4%)
  matrix products  17.1 us (3%)
    another operation x21, other arithmetic, per_device(): diag_factor = jnp.linalg.cholesky(gathered[start:stop])  104 us
    all_gather x3, blocking collectives, gather_panel(): return lax.all_gather(columns, 'wide', axis=0, tiled=True)  97 us
    another operation x14, other arithmetic, per_device(): factor = jnp.linalg.cholesky(block)  87.9 us
    reduce_scatter x1, waiting for transfers between devices, per_device(): local = lax.psum_scatter(summed, 'wide', scatter_dimension=0, tiled=True)  69.1 us
    another operation x7, other arithmetic, lower_solve(): return jax.scipy.linalg.solve_triangular(factor, rows.T, lower=True).T  59.1 us
    ppermute x2, waiting for transfers between devices, per_device(): lax.ppermute(summed, 'scen', [(dev, dev ^ hop) for dev in range(4)])  55.7 us
    another operation x3, other arithmetic, per_device(): jax.scipy.linalg.solve_triangular(factor, coupling * column_mask[:, None,...  39.6 us
    another operation x22, local copies, waits for them, and re-layouts, lower_solve(): return jax.scipy.linalg.solve_triangular(factor, rows.T, lower=True).T  12.1 us
  transfers between devices with their start and end apart: 3, of which 3 were waited for; matrix products, arithmetic and copies ran while one was open for 0% of the time, Pallas kernels for 0%

profile of v1, /device:TPU:0, one launch (start us, length us, event | category | flops | bytes accessed | tf_op | source)
XLA Modules:
  0.0 590.3 jit_solution(14120057107510794168)
XLA Ops:
  9.6 11.7 %custom-call.54 = f32[1,128,128]{2,1,0:T(8,128)S(1)} custom-call(f32[1,128,128]{2,1,0:T(8,128)S(1)} %cholesky.534), custom_call_target="Cholesky" | custom-call | tf_op jit(solution)/shard_map/jit(cholesky)/cholesky | solution.py:33
  21.5 9.8 %custom-call.55 = f32[1,1,128,128]{2,3,1,0:T(8,128)S(1)} custom-call(f32[1,1,128,128]{3,2,1,0:T(8,128)S(1)} %get-tuple-element.194), custom_call_target="InvertDiagBlocksLowerTriangular" | custom-call | tf_op jit(solution)/shard_map/jit(cholesky)/cholesky | solution.py:33
  32.1 11.7 %custom-call.56 = f32[1,128,128]{2,1,0:T(8,128)S(1)} custom-call(f32[1,128,128]{2,1,0:T(8,128)S(1)} %cholesky.538), custom_call_target="Cholesky" | custom-call | tf_op jit(solution)/shard_map/jit(cholesky)/cholesky | solution.py:33
  44.1 10.0 %custom-call.57 = f32[1,1,128,128]{2,3,1,0:T(8,128)S(1)} custom-call(f32[1,1,128,128]{3,2,1,0:T(8,128)S(1)} %get-tuple-element.192), custom_call_target="InvertDiagBlocksLowerTriangular" | custom-call | tf_op jit(solution)/shard_map/jit(cholesky)/cholesky | solution.py:33
  55.1 11.7 %custom-call.58 = f32[1,128,128]{2,1,0:T(8,128)S(1)} custom-call(f32[1,128,128]{2,1,0:T(8,128)S(1)} %cholesky.543), custom_call_target="Cholesky" | custom-call | tf_op jit(solution)/shard_map/jit(cholesky)/cholesky | solution.py:33
  66.9 9.8 %custom-call.59 = f32[1,1,128,128]{2,3,1,0:T(8,128)S(1)} custom-call(f32[1,1,128,128]{3,2,1,0:T(8,128)S(1)} %get-tuple-element.190), custom_call_target="InvertDiagBlocksLowerTriangular" | custom-call | tf_op jit(solution)/shard_map/jit(cholesky)/cholesky | solution.py:33
  77.5 21.0 %custom-call.60 = f32[1,128,128]{2,1,0:T(8,128)S(1)} custom-call(f32[1,128,128]{2,1,0:T(8,128)S(1)} %fusion.18), custom_call_target="Cholesky" | custom-call | tf_op jit(solution)/shard_map/jit(cholesky)/cholesky | solution.py:33
  103.5 8.5 %while.14 = (s32[]{:T(128)}, f32[512,512]{0,1:T(8,128)S(1)}, s32[4,2]{0,1:T(2,128)S(1)}, f32[4,128,128]{2,1,0:T(8,128)S(1)}, s32[]{:T(128)}) while((s32[]{:T(128)}, f32[512,512]{0,1:T(8,128)S(1)}, s32[4,2]{0,1:T(2,128)S(1)}, f32[4,128,128]{2,1,0:T(8,128)S(1)}, s32[]{:T(128)}) %tuple.117), condition=%wide.while_cond.6, body=%wide.while_body.6.sunk | while | flops 2 | bytes 393321 | solution.py:39
  112.0 39.3 %custom-call.61 = f32[4,128,128]{1,2,0:T(8,128)S(1)} custom-call(f32[4,128,128]{2,1,0:T(8,128)S(1)} %get-tuple-element.79), custom_call_target="InvertDiagBlocksLowerTriangular" | custom-call | tf_op jit(solution)/shard_map/jit(_solve_triangular)/triangular_solve | solution.py:39
  157.8 4.5 fusion
  162.9 4.2 collective-permute-done
  167.3 2.9 collective-permute-start.1
  170.2 51.5 %collective-permute-done.1 = f32[768,768]{1,0:T(8,128)S(1)} collective-permute-done((f32[768,768]{1,0:T(8,128)S(1)}, f32[768,768]{1,0:T(8,128)S(1)}, u32[]{:S(2)}, u32[]{:S(2)}) %collective-permute-start.1) | collective-permute-done | bytes 2359328 | tf_op jit(solution)/shard_map/ppermute | solution.py:52
  226.3 69.1 %reduce-scatter.4.cloned.1.call-done = f32[96,768]{1,0:T(8,128)} async-done(((f32[768,768]{1,0:T(8,128)}), f32[96,768]{1,0:T(8,128)}) %reduce-scatter.4.cloned.1.call-update) | async-done | bytes 294928 | tf_op jit(solution)/shard_map/reduce_scatter | solution.py:53
  296.4 32.9 %all_gather.9 = f32[768,256]{1,0:T(8,128)S(1)} all-gather(f32[96,256]{1,0:T(8,128)S(1)} %get-tuple-element.174), channel_id=1, replica_groups=mesh['scen'=4,'wide'=8] {'wide'}, dimensions={0}, use_global_device_ids=true | all-gather | bytes 884736 | tf_op jit(solution)/shard_map/all_gather | solution.py:11
  329.6 11.7 %cholesky.436 = f32[128,128]{1,0:T(8,128)S(1)} custom-call(f32[128,128]{1,0:T(8,128)S(1)} %cholesky.547), custom_call_target="Cholesky" | custom-call | tf_op jit(solution)/shard_map/jit(cholesky)/cholesky | solution.py:64
  341.4 9.8 %custom-call.68 = f32[1,128,128]{1,2,0:T(8,128)S(1)} custom-call(f32[1,128,128]{2,1,0:T(8,128)S(1)} %get-tuple-element.188), custom_call_target="InvertDiagBlocksLowerTriangular" | custom-call | tf_op jit(solution)/shard_map/jit(cholesky)/cholesky | solution.py:64
  351.7 11.7 %cholesky.453 = f32[128,128]{1,0:T(8,128)S(1)} custom-call(f32[128,128]{1,0:T(8,128)S(1)} %convolution_subtract_fusion.7), custom_call_target="Cholesky" | custom-call | tf_op jit(solution)/shard_map/jit(cholesky)/cholesky | solution.py:64
  366.0 4.1 while.15
  370.1 19.7 %custom-call.69 = f32[2,128,128]{1,2,0:T(8,128)S(1)} custom-call(f32[2,128,128]{2,1,0:T(8,128)S(1)} %get-tuple-element.108), custom_call_target="InvertDiagBlocksLowerTriangular" | custom-call | tf_op jit(solution)/shard_map/jit(_solve_triangular)/triangular_solve | solution.py:15
  392.4 32.3 %all_gather.10 = f32[768,256]{1,0:T(8,128)S(1)} all-gather(f32[96,256]{1,0:T(8,128)S(1)} %get-tuple-element.176), channel_id=1, replica_groups=mesh['scen'=4,'wide'=8] {'wide'}, dimensions={0}, use_global_device_ids=true | all-gather | bytes 884736 | tf_op jit(solution)/shard_map/all_gather | solution.py:11
  424.9 11.7 %cholesky.470 = f32[128,128]{1,0:T(8,128)S(1)} custom-call(f32[128,128]{1,0:T(8,128)S(1)} %cholesky.550), custom_call_target="Cholesky" | custom-call | tf_op jit(solution)/shard_map/jit(cholesky)/cholesky | solution.py:64
  436.7 9.8 %custom-call.70 = f32[1,128,128]{1,2,0:T(8,128)S(1)} custom-call(f32[1,128,128]{2,1,0:T(8,128)S(1)} %get-tuple-element.184), custom_call_target="InvertDiagBlocksLowerTriangular" | custom-call | tf_op jit(solution)/shard_map/jit(cholesky)/cholesky | solution.py:64
  446.9 11.7 %cholesky.487 = f32[128,128]{1,0:T(8,128)S(1)} custom-call(f32[128,128]{1,0:T(8,128)S(1)} %convolution_subtract_fusion.6), custom_call_target="Cholesky" | custom-call | tf_op jit(solution)/shard_map/jit(cholesky)/cholesky | solution.py:64
  461.4 4.3 while.16
  465.8 19.7 %custom-call.71 = f32[2,128,128]{1,2,0:T(8,128)S(1)} custom-call(f32[2,128,128]{2,1,0:T(8,128)S(1)} %get-tuple-element.109), custom_call_target="InvertDiagBlocksLowerTriangular" | custom-call | tf_op jit(solution)/shard_map/jit(_solve_triangular)/triangular_solve | solution.py:15
  487.4 31.8 %all_gather.11 = f32[768,256]{1,0:T(8,128)S(1)} all-gather(f32[96,256]{1,0:T(8,128)S(1)} %fusion.16), channel_id=1, replica_groups=mesh['scen'=4,'wide'=8] {'wide'}, dimensions={0}, use_global_device_ids=true | all-gather | bytes 884736 | tf_op jit(solution)/shard_map/all_gather | solution.py:11
  519.4 11.7 %cholesky.504 = f32[128,128]{1,0:T(8,128)S(1)} custom-call(f32[128,128]{1,0:T(8,128)S(1)} %cholesky.553), custom_call_target="Cholesky" | custom-call | tf_op jit(solution)/shard_map/jit(cholesky)/cholesky | solution.py:64
  531.2 9.8 %custom-call.72 = f32[1,128,128]{1,2,0:T(8,128)S(1)} custom-call(f32[1,128,128]{2,1,0:T(8,128)S(1)} %get-tuple-element.180), custom_call_target="InvertDiagBlocksLowerTriangular" | custom-call | tf_op jit(solution)/shard_map/jit(cholesky)/cholesky | solution.py:64
  541.5 11.7 %cholesky.521 = f32[128,128]{1,0:T(8,128)S(1)} custom-call(f32[128,128]{1,0:T(8,128)S(1)} %convolution_subtract_fusion.5), custom_call_target="Cholesky" | custom-call | tf_op jit(solution)/shard_map/jit(cholesky)/cholesky | solution.py:64
  556.0 4.4 while.17
  560.4 19.7 %custom-call.73 = f32[2,128,128]{1,2,0:T(8,128)S(1)} custom-call(f32[2,128,128]{2,1,0:T(8,128)S(1)} %get-tuple-element.110), custom_call_target="InvertDiagBlocksLowerTriangular" | custom-call | tf_op jit(solution)/shard_map/jit(_solve_triangular)/triangular_solve | solution.py:15
  (179 shorter events, 53.8 us)
Async XLA Ops:
  7.2 1.7 copy-start.4
  7.2 1.7 copy-start.5
  7.2 1.7 copy-start.6
  7.2 1.7 copy-start.3
  7.2 1.7 copy-start.2
  7.2 288.2 %reduce-scatter.4.cloned.1.call-start = ((), (), s32[]{:S(2)}) async-start(), calls=%async_computation.1 | async-start | bytes 2654208 | tf_op jit(solution)/shard_map/reduce_scatter | solution.py:53
  103.5 48.5 %copy-start.7 = (s32[1,32]{1,0:T(1,128)S(1)}, s32[1,32]{1,0:T(1,128)}, u32[]{:S(2)}) copy-start(s32[1,32]{1,0:T(1,128)} %param.30) | copy-start | bytes 388
  162.3 4.7 collective-permute-start
  167.3 54.5 %collective-permute-start.1 = (f32[768,768]{1,0:T(8,128)S(1)}, f32[768,768]{1,0:T(8,128)S(1)}, u32[]{:S(2)}, u32[]{:S(2)}) collective-permute-start(f32[768,768]{1,0:T(8,128)S(1)} %add.123), channel_id=1, source_target_pairs={{0,16},{8,24},{16,0},{24,8},{1,17},{9,25},{17,1},{25,9},{2,18},{10... | collective-permute-start | bytes 7077896 | tf_op jit(solution)/shard_map/ppermute | solution.py:52
  223.5 71.9 %copy-start.1 = (f32[96,768]{1,0:T(8,128)S(1)}, f32[96,768]{1,0:T(8,128)}, u32[]{:S(2)}) copy-start(f32[96,768]{1,0:T(8,128)} %param.32) | copy-start | bytes 884740
  329.4 12.0 %copy-start = (f32[768,256]{1,0:T(8,128)}, f32[768,256]{1,0:T(8,128)S(1)}, u32[]{:S(2)}) copy-start(f32[768,256]{1,0:T(8,128)S(1)} %all_gather.9) | copy-start | bytes 2359300
  341.4 48.4 %slice-start = ((f32[768,256]{1,0:T(8,128)}), f32[512,256]{1,0:T(8,128)S(1)}, s32[]{:S(2)}) async-start(f32[768,256]{1,0:T(8,128)} %copy-done), calls=%async_computation.2 | async-start | bytes 1048576 | tf_op jit(solution)/shard_map/slice | solution.py:68
Sparse Core Ops, SparseCore 0:
  223.6 71.7 reduce-scatter.3
